TPU v7x, 512 devices: a whole 4x8x8 slice. The times are simulated.
512 devices in a mesh: sx: 32 (over y_lo, z), sy: 16 (over y_hi, x, core).
Axes of the slice: x: 4, y: 8 (y_hi: 2, y_lo: 4; y = y_hi * 4 + y_lo), z: 8, core: 2. Of those that a mesh axis runs over, the one named last changes fastest.
Arguments:
- right_vectors: bfloat16 [32, 1024, 4096], P(None, 'sx', 'sy'), may hold values from -6 to 6
- left_vectors: bfloat16 [64, 1024, 4096], P(None, 'sx', 'sy'), may hold values from -6 to 6
- classes: int32 [1024, 4096], P('sx', 'sy'), may hold values from 0 to 3
- class_energy: float32 [4], replicated, may hold values from -1.5 to 1.5
- bond_mask_grid: int32 [2, 1024, 4096], P(None, 'sx', 'sy'), may hold values 0 or 1
- order: int32 [5], replicated, may hold values from 0 to 4, each once
Outputs:
- gamma: float32 [5, 64, 32], P(None, 'sy')
Inputs may be any that keep to these rules, and one draw needn't show every extreme that they name: Each order from 0 to 4 appears once.
All inputs are finite; a program needn't handle non-finite values. No bound on the sum of `bond_mask_grid` on one device may be relied on, other than what follows from the above.
Results may differ from a plain program's by a relative error of at most 0.0003.
Values sent between devices are 32-bit elements; how exact they have to be, the bound alone decides.
No kernel may reach another device: no remote copies, remote signals or barrier semaphores. Data moves between devices by JAX's collectives and lax.ppermute only.
A program may use at most 64 MiB of HBM per device.

v0:
```python
import jax
import jax.numpy as jnp
from jax import lax
from jax.sharding import PartitionSpec as P

MOMENTS = 5
half_root = 0.8660254037844386
spectral_scale = 4.6


def shifted(value, axis, by):
    length = lax.axis_size(axis)
    return lax.ppermute(value, axis, [(i, (i + by) % length) for i in range(length)])


def with_halo(value, sides, width):
    for axis, dim in sides:
        size, length = (lax.axis_size(axis), value.shape[dim])
        up = [(i, (i + 1) % size) for i in range(size)]
        down = [(j, i) for i, j in up]
        last = lax.slice_in_dim(value, length - width, length, axis=dim)
        initial = lax.slice_in_dim(value, 0, width, axis=dim)
        before = lax.ppermute(last, axis, up)
        after = lax.ppermute(initial, axis, down)
        value = jnp.concatenate([before, value, after], axis=dim)
    return value


def offsets(padded):
    return (padded[:, 2:, 1:-1], padded[:, :-2, 1:-1], padded[:, 1:-1, 2:], padded[:, 1:-1, :-2])


def shards(right_vectors, left_vectors, classes, class_energy, bond_mask_grid, order):
    rows_x, rows_y = classes.shape
    west_row = shifted(bond_mask_grid[0, -1:, :], "sx", 1)
    south_column = shifted(bond_mask_grid[1, :, -1:], "sy", 1)
    hmask = bond_mask_grid[0].astype(jnp.float32)
    vertical_mask = bond_mask_grid[1].astype(jnp.float32)
    west_mask = jnp.concatenate([west_row.astype(jnp.float32), hmask[:-1]], axis=0)
    south_mask = jnp.concatenate([south_column.astype(jnp.float32), vertical_mask[:, :-1]], axis=1)
    xpos = jnp.arange(rows_x, dtype=jnp.int32)[:, None]
    ypos = jnp.arange(rows_y, dtype=jnp.int32)[None, :]
    sublattice_first = ((xpos + ypos) % 2 == 0).astype(jnp.float32)
    sublattice_second = 1.0 - sublattice_first
    sign = sublattice_first - sublattice_second
    upper_neighbour = vertical_mask * sublattice_first
    lower_neighbour = south_mask * sublattice_second
    energy = jnp.zeros((rows_x, rows_y), jnp.float32)
    for level in range(class_energy.shape[0]):
        energy = energy + (classes == level).astype(jnp.float32) * class_energy[level]

    def beside_all(field):
        return offsets(with_halo(field, (("sx", 1), ("sy", 2)), 1))

    nleft = left_vectors.shape[0]
    nright = right_vectors.shape[0]
    cells = rows_x * rows_y
    left_field = left_vectors.astype(jnp.float32)
    left_flat = left_field.reshape(nleft, cells)
    count = MOMENTS
    moments = []
    u_prev = None
    pe, pw, pn, ps = beside_all(right_vectors.astype(jnp.float32))
    u_now = 0.5 * sign * (hmask * pe + west_mask * pw) - upper_neighbour * pn + lower_neighbour * ps
    for step in range(count):
        final = step == count - 1
        parts = None
        parts = beside_all(u_now)
        vel_pe, vel_pw, vel_pn, vel_ps = parts
        moved = (-half_root * (hmask * vel_pe - west_mask * vel_pw)).reshape(nright, cells)
        moments.append(
            jnp.dot(
                left_flat,
                moved.T,
                precision=lax.Precision.HIGHEST,
                preferred_element_type=jnp.float32,
            )
        )
        if not final:
            hamilton_pe, hamilton_pw, hamilton_pn, hamilton_ps = parts
            image = (
                energy * u_now
                - hmask * hamilton_pe
                - west_mask * hamilton_pw
                - upper_neighbour * hamilton_pn
                - lower_neighbour * hamilton_ps
            ) / spectral_scale
            if step == 0:
                u_next = image
            else:
                u_next = 2.0 * image - u_prev
            u_prev, u_now = (u_now, u_next)
    partial_tiles = jnp.stack(moments)
    owned = nleft // lax.axis_size("sy")
    total = lax.psum(partial_tiles, ("sx", "sy"))
    mine = lax.dynamic_slice_in_dim(total, lax.axis_index("sy") * owned, owned, 1)
    all_sites = cells * lax.axis_size("sx") * lax.axis_size("sy")
    mine = mine * (1.0 / jnp.sqrt(jnp.float32(all_sites)))
    select = (order[:, None] == jnp.arange(count, dtype=jnp.int32)[None, :]).astype(jnp.float32)
    return jnp.einsum("sm,mlr->slr", select, mine, precision=lax.Precision.HIGHEST)


def solution(mesh):
    in_specs = (
        P(None, "sx", "sy"),
        P(None, "sx", "sy"),
        P("sx", "sy"),
        P(),
        P(None, "sx", "sy"),
        P(),
    )
    out_specs = P(None, "sy", None)
    return jax.shard_map(shards, mesh=mesh, in_specs=in_specs, out_specs=out_specs, check_vma=False)
```

profile of v0, /device:TPU:1, one launch (start us, length us, event | category | flops | bytes accessed | tf_op | source)
XLA Modules:
  0.0 309.3 jit_solution(4009982580344775790)
XLA Ops:
  1.5 14.5 %collective-permute-start = (f32[32,1,256]{2,0,1:T(8,128)S(1)}, f32[32,1,256]{2,0,1:T(8,128)S(1)}, u32[]{:S(2)}, u32[]{:S(2)}) collective-permute-start(f32[32,1,256]{2,0,1:T(8,128)S(1)} %get-tuple-element.30), channel_id=1, source_target_pairs={{16,0},{32,16},{48,32},{64,48},{80,64},{96,80},{112,96},{128,112},... | collective-permute-start | bytes 98312 | tf_op jit(solution)/shard_map/ppermute | solution.py:24
  16.0 1.9 collective-permute-start.2
  18.1 4.0 %collective-permute-start.4 = (s32[32,1]{0,1:T(1,128)S(1)}, s32[32,1]{0,1:T(1,128)S(1)}, u32[]{:S(2)}, u32[]{:S(2)}) collective-permute-start(s32[32,1]{0,1:T(1,128)S(1)} %bitcast.60), channel_id=1, source_target_pairs={{0,1},{1,2},{2,3},{3,4},{4,5},{5,6},{6,7},{7,8},{8,9},{9,10},{10,1... | collective-permute-start | bytes 392 | tf_op jit(solution)/shard_map/ppermute | solution.py:13
  22.1 1.9 collective-permute-start.1
  24.3 6.3 %collective-permute-done.1 = s32[1,256]{1,0:T(1,128)S(1)} collective-permute-done((s32[1,256]{1,0:T(1,128)S(1)}, s32[1,256]{1,0:T(1,128)S(1)}, u32[]{:S(2)}, u32[]{:S(2)}) %collective-permute-start.1) | collective-permute-done | bytes 1056 | tf_op jit(solution)/shard_map/ppermute | solution.py:13
  31.4 2.8 collective-permute-start.5
  34.6 1.9 collective-permute-start.3
  37.9 2.0 collective-permute-done.3
  41.3 2.0 fusion.44
  43.3 4.2 %collective-permute-start.6 = (f32[32,1,256]{2,0,1:T(8,128)S(1)}, f32[32,1,256]{2,0,1:T(8,128)S(1)}, u32[]{:S(2)}, u32[]{:S(2)}) collective-permute-start(f32[32,1,256]{2,0,1:T(8,128)S(1)} %get-tuple-element.28), channel_id=1, source_target_pairs={{16,0},{32,16},{48,32},{64,48},{80,64},{96,80},{112,96},{128,112},... | collective-permute-start | bytes 98312 | tf_op jit(solution)/shard_map/ppermute | solution.py:24
  47.5 1.9 collective-permute-start.7
  50.1 6.0 %collective-permute-done.7 = f32[32,1,256]{2,0,1:T(8,128)S(1)} collective-permute-done((f32[32,1,256]{2,0,1:T(8,128)S(1)}, f32[32,1,256]{2,0,1:T(8,128)S(1)}, u32[]{:S(2)}, u32[]{:S(2)}) %collective-permute-start.7) | collective-permute-done | bytes 32800 | tf_op jit(solution)/shard_map/ppermute | solution.py:23
  58.8 2.5 collective-permute-start.9
  62.7 10.5 %collective-permute-start.8 = (f32[32,34,1]{1,0,2:T(8,128)S(1)}, f32[32,34,1]{1,0,2:T(8,128)}, u32[]{:S(2)}, u32[]{:S(2)}) collective-permute-start(f32[32,34,1]{1,0,2:T(8,128)S(1)} %copy.129), channel_id=1, source_target_pairs={{1,0},{2,1},{3,2},{4,3},{5,4},{6,5},{7,6},{8,7},{9,8},{10,9},{11,1... | collective-permute-start | bytes 13064 | tf_op jit(solution)/shard_map/ppermute | solution.py:24
  73.2 3.2 %broadcast_multiply_fusion.1 = (f32[32,256]{1,0:T(8,128)}, f32[32,256]{1,0:T(8,128)S(1)}) fusion(f32[]{:T(128)} %bitcast.12, s32[32,256]{1,0:T(8,128)S(1)} %copy-done.25, f32[]{:T(128)} %bitcast.11, f32[]{:T(128)} %bitcast.10, f32[]{:T(128)} %bitcast.9), kind=kLoop, calls=%fused_computation.158 | loop fusion | flops 98304 | bytes 98320 | tf_op jit(solution)/shard_map/mul | solution.py:82
  77.8 2.1 copy.92
  79.9 2.9 broadcast_multiply_fusion
  82.9 1.9 collective-permute-start.10
  84.8 3.4 %collective-permute-start.11 = (f32[32,1,256]{2,0,1:T(8,128)S(1)}, f32[32,1,256]{2,0,1:T(8,128)S(1)}, u32[]{:S(2)}, u32[]{:S(2)}) collective-permute-start(f32[32,1,256]{2,0,1:T(8,128)S(1)} %get-tuple-element.25), channel_id=1, source_target_pairs={{0,16},{16,32},{32,48},{48,64},{64,80},{80,96},{96,112},{112,128},... | collective-permute-start | bytes 98312 | tf_op jit(solution)/shard_map/ppermute | solution.py:23
  88.2 5.2 %collective-permute-done.11 = f32[32,1,256]{2,0,1:T(8,128)S(1)} collective-permute-done((f32[32,1,256]{2,0,1:T(8,128)S(1)}, f32[32,1,256]{2,0,1:T(8,128)S(1)}, u32[]{:S(2)}, u32[]{:S(2)}) %collective-permute-start.11) | collective-permute-done | bytes 32800 | tf_op jit(solution)/shard_map/ppermute | solution.py:23
  94.1 2.0 collective-permute-start.13
  96.6 10.8 %collective-permute-start.12 = (f32[32,34,1]{1,0,2:T(8,128)S(1)}, f32[32,34,1]{1,0,2:T(8,128)S(1)}, u32[]{:S(2)}, u32[]{:S(2)}) collective-permute-start(f32[32,34,1]{1,0,2:T(8,128)S(1)} %copy.131), channel_id=1, source_target_pairs={{1,0},{2,1},{3,2},{4,3},{5,4},{6,5},{7,6},{8,7},{9,8},{10,9},{11,1... | collective-permute-start | bytes 13064 | tf_op jit(solution)/shard_map/ppermute | solution.py:24
  110.1 5.8 %fusion.32 = f32[32,32,256]{2,0,1:T(8,128)S(1)} fusion(f32[32,34,1]{2,0,1:T(8,128)} %copy.100, f32[32,1,256]{2,0,1:T(8,128)S(1)} %collective-permute-done.10, f32[32,32,256]{2,0,1:T(8,128)} %copy-done.1, f32[32,1,256]{2,0,1:T(8,128)S(1)} %collective-permute-done.11, f32[32,34,1]{2,0,1:T(8,128)} %copy.98, f32[32,32,256]{2,0,1:T(8,128)} %get-tuple-element.8, ...), kind=kLoop, calls=%fused_computation.59 | loop fusion | flops 9175040 | bytes 4539392 | tf_op jit(solution)/shard_map/sub | solution.py:91
  115.9 1.9 collective-permute-start.14
  117.8 3.4 %collective-permute-start.15 = (f32[32,1,256]{2,0,1:T(8,128)S(1)}, f32[32,1,256]{2,0,1:T(8,128)S(1)}, u32[]{:S(2)}, u32[]{:S(2)}) collective-permute-start(f32[32,1,256]{2,0,1:T(8,128)S(1)} %get-tuple-element.23), channel_id=1, source_target_pairs={{0,16},{16,32},{32,48},{48,64},{64,80},{80,96},{96,112},{112,128},... | collective-permute-start | bytes 98312 | tf_op jit(solution)/shard_map/ppermute | solution.py:23
  121.2 5.2 %collective-permute-done.15 = f32[32,1,256]{2,0,1:T(8,128)S(1)} collective-permute-done((f32[32,1,256]{2,0,1:T(8,128)S(1)}, f32[32,1,256]{2,0,1:T(8,128)S(1)}, u32[]{:S(2)}, u32[]{:S(2)}) %collective-permute-start.15) | collective-permute-done | bytes 32800 | tf_op jit(solution)/shard_map/ppermute | solution.py:23
  129.7 1.9 collective-permute-start.17
  131.6 2.0 copy.133
  133.7 11.0 %collective-permute-start.16 = (f32[32,34,1]{1,0,2:T(8,128)}, f32[32,34,1]{1,0,2:T(8,128)}, u32[]{:S(2)}, u32[]{:S(2)}) collective-permute-start(f32[32,34,1]{1,0,2:T(8,128)} %copy.133), channel_id=1, source_target_pairs={{1,0},{2,1},{3,2},{4,3},{5,4},{6,5},{7,6},{8,7},{9,8},{10,9},{11,1... | collective-permute-start | bytes 13064 | tf_op jit(solution)/shard_map/ppermute | solution.py:24
  144.7 2.1 fusion.4
  146.8 2.1 copy.106
  148.9 2.1 copy.104
  151.0 2.4 fusion.24
  153.4 1.9 collective-permute-start.18
  155.4 3.4 %collective-permute-start.19 = (f32[32,1,256]{2,0,1:T(8,128)S(1)}, f32[32,1,256]{2,0,1:T(8,128)S(1)}, u32[]{:S(2)}, u32[]{:S(2)}) collective-permute-start(f32[32,1,256]{2,0,1:T(8,128)S(1)} %get-tuple-element.21), channel_id=1, source_target_pairs={{0,16},{16,32},{32,48},{48,64},{64,80},{80,96},{96,112},{112,128},... | collective-permute-start | bytes 98312 | tf_op jit(solution)/shard_map/ppermute | solution.py:23
  158.8 2.2 fusion.3
  161.0 3.0 collective-permute-done.19
  167.0 1.9 collective-permute-start.21
  170.0 10.8 %collective-permute-start.20 = (f32[32,34,1]{1,0,2:T(8,128)}, f32[32,34,1]{1,0,2:T(8,128)}, u32[]{:S(2)}, u32[]{:S(2)}) collective-permute-start(f32[32,34,1]{1,0,2:T(8,128)} %copy.135), channel_id=1, source_target_pairs={{1,0},{2,1},{3,2},{4,3},{5,4},{6,5},{7,6},{8,7},{9,8},{10,9},{11,1... | collective-permute-start | bytes 13064 | tf_op jit(solution)/shard_map/ppermute | solution.py:24
  180.8 2.1 fusion.2
  182.9 2.2 copy.112
  185.1 2.1 copy.110
  187.1 1.9 fusion.16
  189.1 1.9 collective-permute-start.23
  191.0 7.5 %collective-permute-start.22 = (f32[32,1,256]{2,0,1:T(8,128)S(1)}, f32[32,1,256]{2,0,1:T(8,128)S(1)}, u32[]{:S(2)}, u32[]{:S(2)}) collective-permute-start(f32[32,1,256]{2,0,1:T(8,128)S(1)} %get-tuple-element.19), channel_id=1, source_target_pairs={{16,0},{32,16},{48,32},{64,48},{80,64},{96,80},{112,96},{128,112},... | collective-permute-start | bytes 98312 | tf_op jit(solution)/shard_map/ppermute | solution.py:24
  198.5 2.1 fusion.1
  200.7 2.2 fusion
  202.8 105.7 %psum.7 = f32[5,64,32]{2,1,0:T(8,128)S(1)} all-reduce(f32[5,64,32]{2,1,0:T(8,128)S(1)} %fusion), channel_id=1, replica_groups=mesh['sx'=32,'sy'=16] {'sx','sy'}, use_global_device_ids=true, to_apply=%region_0.1 | all-reduce | flops 10240 | bytes 81920 | tf_op jit(solution)/shard_map/psum | solution.py:95
  (119 shorter events, 24.1 us)
Async XLA Ops:
  0.0 144.7 %copy-start = (bf16[64,32,256]{2,1,0:T(8,128)(2,1)S(1)}, bf16[64,32,256]{2,1,0:T(8,128)(2,1)}, u32[]{:S(2)}) copy-start(bf16[64,32,256]{2,1,0:T(8,128)(2,1)} %param.7) | copy-start | bytes 3145732
  0.0 17.9 %copy-start.7 = (s32[2,32,256]{2,1,0:T(8,128)S(1)}, s32[2,32,256]{2,1,0:T(8,128)}, u32[]{:S(2)}) copy-start(s32[2,32,256]{2,1,0:T(8,128)} %param.10) | copy-start | bytes 196612
  1.5 29.1 %collective-permute-start = (f32[32,1,256]{2,0,1:T(8,128)S(1)}, f32[32,1,256]{2,0,1:T(8,128)S(1)}, u32[]{:S(2)}, u32[]{:S(2)}) collective-permute-start(f32[32,1,256]{2,0,1:T(8,128)S(1)} %get-tuple-element.30), channel_id=1, source_target_pairs={{16,0},{32,16},{48,32},{64,48},{80,64},{96,80},{112,96},{128,112},... | collective-permute-start | bytes 98312 | tf_op jit(solution)/shard_map/ppermute | solution.py:24
  16.0 14.6 %collective-permute-start.2 = (f32[32,1,256]{2,0,1:T(8,128)S(1)}, f32[32,1,256]{2,0,1:T(8,128)S(1)}, u32[]{:S(2)}, u32[]{:S(2)}) collective-permute-start(f32[32,1,256]{2,0,1:T(8,128)S(1)} %get-tuple-element.29), channel_id=1, source_target_pairs={{0,16},{16,32},{32,48},{48,64},{64,80},{80,96},{96,112},{112,128},... | collective-permute-start | bytes 98312 | tf_op jit(solution)/shard_map/ppermute | solution.py:23
  18.1 6.0 %collective-permute-start.4 = (s32[32,1]{0,1:T(1,128)S(1)}, s32[32,1]{0,1:T(1,128)S(1)}, u32[]{:S(2)}, u32[]{:S(2)}) collective-permute-start(s32[32,1]{0,1:T(1,128)S(1)} %bitcast.60), channel_id=1, source_target_pairs={{0,1},{1,2},{2,3},{3,4},{4,5},{5,6},{6,7},{7,8},{8,9},{9,10},{10,1... | collective-permute-start | bytes 392 | tf_op jit(solution)/shard_map/ppermute | solution.py:13
  22.1 8.5 %collective-permute-start.1 = (s32[1,256]{1,0:T(1,128)S(1)}, s32[1,256]{1,0:T(1,128)S(1)}, u32[]{:S(2)}, u32[]{:S(2)}) collective-permute-start(s32[1,256]{1,0:T(1,128)S(1)} %slice_bitcast_fusion.1), channel_id=1, source_target_pairs={{0,16},{16,32},{32,48},{48,64},{64,80},{80,96},{96,112},{112,128},... | collective-permute-start | bytes 3080 | tf_op jit(solution)/shard_map/ppermute | solution.py:13
  31.4 5.1 %collective-permute-start.5 = (f32[32,34,1]{1,0,2:T(8,128)S(1)}, f32[32,34,1]{1,0,2:T(8,128)S(1)}, u32[]{:S(2)}, u32[]{:S(2)}) collective-permute-start(f32[32,34,1]{1,0,2:T(8,128)S(1)} %copy.128), channel_id=1, source_target_pairs={{0,1},{1,2},{2,3},{3,4},{4,5},{5,6},{6,7},{7,8},{8,9},{9,10},{10,1... | collective-permute-start | bytes 13064 | tf_op jit(solution)/shard_map/ppermute | solution.py:23
  34.6 5.3 %collective-permute-start.3 = (f32[32,34,1]{1,0,2:T(8,128)S(1)}, f32[32,34,1]{1,0,2:T(8,128)S(1)}, u32[]{:S(2)}, u32[]{:S(2)}) collective-permute-start(f32[32,34,1]{1,0,2:T(8,128)S(1)} %copy.127), channel_id=1, source_target_pairs={{1,0},{2,1},{3,2},{4,3},{5,4},{6,5},{7,6},{8,7},{9,8},{10,9},{11,1... | collective-permute-start | bytes 13064 | tf_op jit(solution)/shard_map/ppermute | solution.py:24
  41.3 8.1 %copy-start.26 = (f32[4]{0:T(128)S(1)}, f32[4]{0:T(128)}, u32[]{:S(2)}) copy-start(f32[4]{0:T(128)} %param.9) | copy-start | bytes 52
  43.3 36.6 %copy-start.5 = (f32[32,32,256]{2,0,1:T(8,128)}, f32[32,32,256]{2,0,1:T(8,128)S(1)}, u32[]{:S(2)}) copy-start(f32[32,32,256]{2,0,1:T(8,128)S(1)} %fusion.44) | copy-start | bytes 3145732
  43.3 6.8 %collective-permute-start.6 = (f32[32,1,256]{2,0,1:T(8,128)S(1)}, f32[32,1,256]{2,0,1:T(8,128)S(1)}, u32[]{:S(2)}, u32[]{:S(2)}) collective-permute-start(f32[32,1,256]{2,0,1:T(8,128)S(1)} %get-tuple-element.28), channel_id=1, source_target_pairs={{16,0},{32,16},{48,32},{64,48},{80,64},{96,80},{112,96},{128,112},... | collective-permute-start | bytes 98312 | tf_op jit(solution)/shard_map/ppermute | solution.py:24
  47.5 8.6 %collective-permute-start.7 = (f32[32,1,256]{2,0,1:T(8,128)S(1)}, f32[32,1,256]{2,0,1:T(8,128)S(1)}, u32[]{:S(2)}, u32[]{:S(2)}) collective-permute-start(f32[32,1,256]{2,0,1:T(8,128)S(1)} %get-tuple-element.27), channel_id=1, source_target_pairs={{0,16},{16,32},{32,48},{48,64},{64,80},{80,96},{96,112},{112,128},... | collective-permute-start | bytes 98312 | tf_op jit(solution)/shard_map/ppermute | solution.py:23
  50.1 29.8 %copy-start.8 = (f32[32,1,256]{2,0,1:T(8,128)}, f32[32,1,256]{2,0,1:T(8,128)S(1)}, u32[]{:S(2)}) copy-start(f32[32,1,256]{2,0,1:T(8,128)S(1)} %collective-permute-done.6) | copy-start | bytes 98308
  56.0 23.9 %copy-start.10 = (f32[32,1,256]{2,0,1:T(8,128)}, f32[32,1,256]{2,0,1:T(8,128)S(1)}, u32[]{:S(2)}) copy-start(f32[32,1,256]{2,0,1:T(8,128)S(1)} %collective-permute-done.7) | copy-start | bytes 98308
  57.3 15.9 %copy-start.25 = (s32[32,256]{1,0:T(8,128)S(1)}, s32[32,256]{1,0:T(8,128)}, u32[]{:S(2)}) copy-start(s32[32,256]{1,0:T(8,128)} %param.8) | copy-start | bytes 98308
  58.8 17.7 %collective-permute-start.9 = (f32[32,34,1]{1,0,2:T(8,128)S(1)}, f32[32,34,1]{1,0,2:T(8,128)S(1)}, u32[]{:S(2)}, u32[]{:S(2)}) collective-permute-start(f32[32,34,1]{1,0,2:T(8,128)S(1)} %copy.130), channel_id=1, source_target_pairs={{0,1},{1,2},{2,3},{3,4},{4,5},{5,6},{6,7},{7,8},{8,9},{9,10},{10,1... | collective-permute-start | bytes 13064 | tf_op jit(solution)/shard_map/ppermute | solution.py:23
  62.7 15.1 %collective-permute-start.8 = (f32[32,34,1]{1,0,2:T(8,128)S(1)}, f32[32,34,1]{1,0,2:T(8,128)}, u32[]{:S(2)}, u32[]{:S(2)}) collective-permute-start(f32[32,34,1]{1,0,2:T(8,128)S(1)} %copy.129), channel_id=1, source_target_pairs={{1,0},{2,1},{3,2},{4,3},{5,4},{6,5},{7,6},{8,7},{9,8},{10,9},{11,1... | collective-permute-start | bytes 13064 | tf_op jit(solution)/shard_map/ppermute | solution.py:24
  82.8 10.6 %copy-start.1 = (f32[32,32,256]{2,0,1:T(8,128)}, f32[32,32,256]{2,0,1:T(8,128)S(1)}, u32[]{:S(2)}) copy-start(f32[32,32,256]{2,0,1:T(8,128)S(1)} %get-tuple-element.7) | copy-start | bytes 3145732
  82.9 5.3 %collective-permute-start.10 = (f32[32,1,256]{2,0,1:T(8,128)S(1)}, f32[32,1,256]{2,0,1:T(8,128)S(1)}, u32[]{:S(2)}, u32[]{:S(2)}) collective-permute-start(f32[32,1,256]{2,0,1:T(8,128)S(1)} %get-tuple-element.26), channel_id=1, source_target_pairs={{16,0},{32,16},{48,32},{64,48},{80,64},{96,80},{112,96},{128,112},... | collective-permute-start | bytes 98312 | tf_op jit(solution)/shard_map/ppermute | solution.py:24
  84.8 8.6 %collective-permute-start.11 = (f32[32,1,256]{2,0,1:T(8,128)S(1)}, f32[32,1,256]{2,0,1:T(8,128)S(1)}, u32[]{:S(2)}, u32[]{:S(2)}) collective-permute-start(f32[32,1,256]{2,0,1:T(8,128)S(1)} %get-tuple-element.25), channel_id=1, source_target_pairs={{0,16},{16,32},{32,48},{48,64},{64,80},{80,96},{96,112},{112,128},... | collective-permute-start | bytes 98312 | tf_op jit(solution)/shard_map/ppermute | solution.py:23
  88.2 21.9 %copy-start.12 = (f32[32,1,256]{2,0,1:T(8,128)}, f32[32,1,256]{2,0,1:T(8,128)S(1)}, u32[]{:S(2)}) copy-start(f32[32,1,256]{2,0,1:T(8,128)S(1)} %collective-permute-done.10) | copy-start | bytes 98308
  93.4 16.7 %copy-start.14 = (f32[32,1,256]{2,0,1:T(8,128)}, f32[32,1,256]{2,0,1:T(8,128)S(1)}, u32[]{:S(2)}) copy-start(f32[32,1,256]{2,0,1:T(8,128)S(1)} %collective-permute-done.11) | copy-start | bytes 98308
  94.1 16.0 %copy-start.24 = (f32[32,256]{1,0:T(8,128)S(1)}, f32[32,256]{1,0:T(8,128)}, u32[]{:S(2)}) copy-start(f32[32,256]{1,0:T(8,128)} %get-tuple-element.5) | copy-start | bytes 98308
  94.1 13.3 %collective-permute-start.13 = (f32[32,34,1]{1,0,2:T(8,128)S(1)}, f32[32,34,1]{1,0,2:T(8,128)S(1)}, u32[]{:S(2)}, u32[]{:S(2)}) collective-permute-start(f32[32,34,1]{1,0,2:T(8,128)S(1)} %copy.132), channel_id=1, source_target_pairs={{0,1},{1,2},{2,3},{3,4},{4,5},{5,6},{6,7},{7,8},{8,9},{9,10},{10,1... | collective-permute-start | bytes 13064 | tf_op jit(solution)/shard_map/ppermute | solution.py:23
  96.6 12.2 %collective-permute-start.12 = (f32[32,34,1]{1,0,2:T(8,128)S(1)}, f32[32,34,1]{1,0,2:T(8,128)S(1)}, u32[]{:S(2)}, u32[]{:S(2)}) collective-permute-start(f32[32,34,1]{1,0,2:T(8,128)S(1)} %copy.131), channel_id=1, source_target_pairs={{1,0},{2,1},{3,2},{4,3},{5,4},{6,5},{7,6},{8,7},{9,8},{10,9},{11,1... | collective-permute-start | bytes 13064 | tf_op jit(solution)/shard_map/ppermute | solution.py:24
  115.9 5.3 %collective-permute-start.14 = (f32[32,1,256]{2,0,1:T(8,128)S(1)}, f32[32,1,256]{2,0,1:T(8,128)S(1)}, u32[]{:S(2)}, u32[]{:S(2)}) collective-permute-start(f32[32,1,256]{2,0,1:T(8,128)S(1)} %get-tuple-element.24), channel_id=1, source_target_pairs={{16,0},{32,16},{48,32},{64,48},{80,64},{96,80},{112,96},{128,112},... | collective-permute-start | bytes 98312 | tf_op jit(solution)/shard_map/ppermute | solution.py:24
  117.8 8.6 %collective-permute-start.15 = (f32[32,1,256]{2,0,1:T(8,128)S(1)}, f32[32,1,256]{2,0,1:T(8,128)S(1)}, u32[]{:S(2)}, u32[]{:S(2)}) collective-permute-start(f32[32,1,256]{2,0,1:T(8,128)S(1)} %get-tuple-element.23), channel_id=1, source_target_pairs={{0,16},{16,32},{32,48},{48,64},{64,80},{80,96},{96,112},{112,128},... | collective-permute-start | bytes 98312 | tf_op jit(solution)/shard_map/ppermute | solution.py:23
  121.2 5.3 %copy-start.16 = (f32[32,1,256]{2,0,1:T(8,128)}, f32[32,1,256]{2,0,1:T(8,128)S(1)}, u32[]{:S(2)}) copy-start(f32[32,1,256]{2,0,1:T(8,128)S(1)} %collective-permute-done.14) | copy-start | bytes 98308
  128.2 16.5 %copy-start.6 = (f32[32,32,256]{2,0,1:T(8,128)S(1)}, f32[32,32,256]{2,0,1:T(8,128)}, u32[]{:S(2)}) copy-start(f32[32,32,256]{2,0,1:T(8,128)} %copy-done.5) | copy-start | bytes 3145732
  128.2 16.5 %copy-start.9 = (f32[32,1,256]{2,0,1:T(8,128)S(1)}, f32[32,1,256]{2,0,1:T(8,128)}, u32[]{:S(2)}) copy-start(f32[32,1,256]{2,0,1:T(8,128)} %copy-done.8) | copy-start | bytes 98308
  128.2 16.5 %copy-start.11 = (f32[32,1,256]{2,0,1:T(8,128)S(1)}, f32[32,1,256]{2,0,1:T(8,128)}, u32[]{:S(2)}) copy-start(f32[32,1,256]{2,0,1:T(8,128)} %copy-done.10) | copy-start | bytes 98308
  129.7 17.1 %collective-permute-start.17 = (f32[32,34,1]{1,0,2:T(8,128)S(1)}, f32[32,34,1]{1,0,2:T(8,128)}, u32[]{:S(2)}, u32[]{:S(2)}) collective-permute-start(f32[32,34,1]{1,0,2:T(8,128)S(1)} %copy.134), channel_id=1, source_target_pairs={{0,1},{1,2},{2,3},{3,4},{4,5},{5,6},{6,7},{7,8},{8,9},{9,10},{10,1... | collective-permute-start | bytes 13064 | tf_op jit(solution)/shard_map/ppermute | solution.py:23
  133.7 15.3 %collective-permute-start.16 = (f32[32,34,1]{1,0,2:T(8,128)}, f32[32,34,1]{1,0,2:T(8,128)}, u32[]{:S(2)}, u32[]{:S(2)}) collective-permute-start(f32[32,34,1]{1,0,2:T(8,128)} %copy.133), channel_id=1, source_target_pairs={{1,0},{2,1},{3,2},{4,3},{5,4},{6,5},{7,6},{8,7},{9,8},{10,9},{11,1... | collective-permute-start | bytes 13064 | tf_op jit(solution)/shard_map/ppermute | solution.py:24
  151.0 7.8 %copy-start.2 = (f32[32,32,256]{2,0,1:T(8,128)S(1)}, f32[32,32,256]{2,0,1:T(8,128)}, u32[]{:S(2)}) copy-start(f32[32,32,256]{2,0,1:T(8,128)} %copy-done.1) | copy-start | bytes 3145732
  151.0 7.8 %copy-start.13 = (f32[32,1,256]{2,0,1:T(8,128)S(1)}, f32[32,1,256]{2,0,1:T(8,128)}, u32[]{:S(2)}) copy-start(f32[32,1,256]{2,0,1:T(8,128)} %copy-done.12) | copy-start | bytes 98308
  151.0 7.8 %copy-start.15 = (f32[32,1,256]{2,0,1:T(8,128)S(1)}, f32[32,1,256]{2,0,1:T(8,128)}, u32[]{:S(2)}) copy-start(f32[32,1,256]{2,0,1:T(8,128)} %copy-done.14) | copy-start | bytes 98308
  153.4 10.5 %copy-start.3 = (f32[32,32,256]{2,0,1:T(8,128)}, f32[32,32,256]{2,0,1:T(8,128)S(1)}, u32[]{:S(2)}) copy-start(f32[32,32,256]{2,0,1:T(8,128)S(1)} %fusion.24) | copy-start | bytes 3145732
  153.4 7.5 %collective-permute-start.18 = (f32[32,1,256]{2,0,1:T(8,128)S(1)}, f32[32,1,256]{2,0,1:T(8,128)S(1)}, u32[]{:S(2)}, u32[]{:S(2)}) collective-permute-start(f32[32,1,256]{2,0,1:T(8,128)S(1)} %get-tuple-element.22), channel_id=1, source_target_pairs={{16,0},{32,16},{48,32},{64,48},{80,64},{96,80},{112,96},{128,112},... | collective-permute-start | bytes 98312 | tf_op jit(solution)/shard_map/ppermute | solution.py:24
  155.4 8.6 %collective-permute-start.19 = (f32[32,1,256]{2,0,1:T(8,128)S(1)}, f32[32,1,256]{2,0,1:T(8,128)S(1)}, u32[]{:S(2)}, u32[]{:S(2)}) collective-permute-start(f32[32,1,256]{2,0,1:T(8,128)S(1)} %get-tuple-element.21), channel_id=1, source_target_pairs={{0,16},{16,32},{32,48},{48,64},{64,80},{80,96},{96,112},{112,128},... | collective-permute-start | bytes 98312 | tf_op jit(solution)/shard_map/ppermute | solution.py:23
  165.6 15.2 %copy-start.17 = (f32[32,1,256]{2,0,1:T(8,128)S(1)}, f32[32,1,256]{2,0,1:T(8,128)}, u32[]{:S(2)}) copy-start(f32[32,1,256]{2,0,1:T(8,128)} %copy-done.16) | copy-start | bytes 98308
  165.6 15.2 %copy-start.19 = (f32[32,1,256]{2,0,1:T(8,128)S(1)}, f32[32,1,256]{2,0,1:T(8,128)}, u32[]{:S(2)}) copy-start(f32[32,1,256]{2,0,1:T(8,128)} %copy-done.18) | copy-start | bytes 98308
  167.0 15.9 %collective-permute-start.21 = (f32[32,34,1]{1,0,2:T(8,128)S(1)}, f32[32,34,1]{1,0,2:T(8,128)}, u32[]{:S(2)}, u32[]{:S(2)}) collective-permute-start(f32[32,34,1]{1,0,2:T(8,128)S(1)} %copy.136), channel_id=1, source_target_pairs={{0,1},{1,2},{2,3},{3,4},{4,5},{5,6},{6,7},{7,8},{8,9},{9,10},{10,1... | collective-permute-start | bytes 13064 | tf_op jit(solution)/shard_map/ppermute | solution.py:23
  170.0 15.1 %collective-permute-start.20 = (f32[32,34,1]{1,0,2:T(8,128)}, f32[32,34,1]{1,0,2:T(8,128)}, u32[]{:S(2)}, u32[]{:S(2)}) collective-permute-start(f32[32,34,1]{1,0,2:T(8,128)} %copy.135), channel_id=1, source_target_pairs={{1,0},{2,1},{3,2},{4,3},{5,4},{6,5},{7,6},{8,7},{9,8},{10,9},{11,1... | collective-permute-start | bytes 13064 | tf_op jit(solution)/shard_map/ppermute | solution.py:24
  182.9 4.3 %copy-start.4 = (f32[32,32,256]{2,0,1:T(8,128)S(1)}, f32[32,32,256]{2,0,1:T(8,128)}, u32[]{:S(2)}) copy-start(f32[32,32,256]{2,0,1:T(8,128)} %copy-done.3) | copy-start | bytes 3145732
  182.9 4.3 %copy-start.21 = (f32[32,1,256]{2,0,1:T(8,128)S(1)}, f32[32,1,256]{2,0,1:T(8,128)}, u32[]{:S(2)}) copy-start(f32[32,1,256]{2,0,1:T(8,128)} %copy-done.20) | copy-start | bytes 98308
  189.1 11.5 %collective-permute-start.23 = (f32[32,1,256]{2,0,1:T(8,128)S(1)}, f32[32,1,256]{2,0,1:T(8,128)S(1)}, u32[]{:S(2)}, u32[]{:S(2)}) collective-permute-start(f32[32,1,256]{2,0,1:T(8,128)S(1)} %get-tuple-element.20), channel_id=1, source_target_pairs={{0,16},{16,32},{32,48},{48,64},{64,80},{80,96},{96,112},{112,128},... | collective-permute-start | bytes 98312 | tf_op jit(solution)/shard_map/ppermute | solution.py:23
  191.0 9.6 %collective-permute-start.22 = (f32[32,1,256]{2,0,1:T(8,128)S(1)}, f32[32,1,256]{2,0,1:T(8,128)S(1)}, u32[]{:S(2)}, u32[]{:S(2)}) collective-permute-start(f32[32,1,256]{2,0,1:T(8,128)S(1)} %get-tuple-element.19), channel_id=1, source_target_pairs={{16,0},{32,16},{48,32},{64,48},{80,64},{96,80},{112,96},{128,112},... | collective-permute-start | bytes 98312 | tf_op jit(solution)/shard_map/ppermute | solution.py:24
  200.6 107.9 %copy-start.27 = (s32[5]{0:T(128)S(1)}, s32[5]{0:T(128)}, u32[]{:S(2)}) copy-start(s32[5]{0:T(128)} %param.11) | copy-start | bytes 64
  (4 other events, 8.6 us)
where the time goes:
time: 311 us; the launch traced here: 309 us
  starting transfers between devices  110 us (35%)
  blocking collectives  106 us (34%)
  local copies, waits for them, and re-layouts  34.3 us (11%)
  waiting for transfers between devices  27.7 us (9%)
  other arithmetic  20.3 us (7%)
  matrix products  10.8 us (3%)
    psum x1, blocking collectives, shards(): total = lax.psum(partial_tiles, ('sx', 'sy'))  106 us
    ppermute x11, starting transfers between devices, with_halo(): after = lax.ppermute(initial, axis, down)  76.9 us
    ppermute x11, starting transfers between devices, with_halo(): before = lax.ppermute(last, axis, up)  27 us
    ppermute x11, waiting for transfers between devices, with_halo(): before = lax.ppermute(last, axis, up)  19.3 us
    unnamed x66, local copies, waits for them, and re-layouts  11.6 us
    dot_general x5, matrix products, shards(): jnp.dot(left_flat, moved.T, precision=lax.Precision.HIGHEST, preferred_el...  10.6 us
    sub x3, other arithmetic, shards(): u_next = 2.0 * image - u_prev  10.2 us
    ppermute x5, local copies, waits for them, and re-layouts, with_halo(): after = lax.ppermute(initial, axis, down)  8.93 us
  transfers between devices with their start and end apart: 24, of which 6 were waited for; matrix products, arithmetic and copies ran while one was open for 9% of the time, Pallas kernels for 0%

commit v1 on v0

--- a/solution.py
+++ b/solution.py
@@ -92,7 +92,7 @@
             u_prev, u_now = (u_now, u_next)
     partial_tiles = jnp.stack(moments)
     owned = nleft // lax.axis_size("sy")
-    total = lax.psum(partial_tiles, ("sx", "sy"))
+    total = lax.psum(lax.psum(partial_tiles, "sx"), "sy")
     mine = lax.dynamic_slice_in_dim(total, lax.axis_index("sy") * owned, owned, 1)
     all_sites = cells * lax.axis_size("sx") * lax.axis_size("sy")
     mine = mine * (1.0 / jnp.sqrt(jnp.float32(all_sites)))

time: 311 us -> 450 us (1.45)
  blocking collectives: 106 us -> 240 us
    psum x1 -> x2, blocking collectives: 106 us -> 240 us  [shards(): total = lax.psum(lax.psum(partial_tiles, 'sx'), 'sy')]
    unnamed x66 -> x62, local copies, waits for them, and re-layouts: 11.6 us -> 12.6 us
  transfers between devices with their start and end apart: 24 -> 24, of which waited for: 6 -> 6; matrix products, arithmetic and copies ran while one was open for 9% -> 6% of each run, Pallas kernels for 0% -> 0%
where the time goes in v1:
time: 450 us; the launch traced here: 444 us
  blocking collectives  240 us (53%)
  starting transfers between devices  110 us (24%)
  local copies, waits for them, and re-layouts  35.3 us (8%)
  waiting for transfers between devices  27.8 us (6%)
  other arithmetic  20.2 us (4%)
  matrix products  10.8 us (2%)
    psum x2, blocking collectives, shards(): total = lax.psum(lax.psum(partial_tiles, 'sx'), 'sy')  240 us
    ppermute x11, starting transfers between devices, with_halo(): after = lax.ppermute(initial, axis, down)  76.9 us
    ppermute x11, starting transfers between devices, with_halo(): before = lax.ppermute(last, axis, up)  27 us
    ppermute x11, waiting for transfers between devices, with_halo(): before = lax.ppermute(last, axis, up)  19.4 us
    unnamed x62, local copies, waits for them, and re-layouts  12.6 us
    dot_general x5, matrix products, shards(): jnp.dot(left_flat, moved.T, precision=lax.Precision.HIGHEST, preferred_el...  10.6 us
    sub x3, other arithmetic, shards(): u_next = 2.0 * image - u_prev  10.3 us
  transfers between devices with their start and end apart: 24, of which 6 were waited for; matrix products, arithmetic and copies ran while one was open for 6% of the time, Pallas kernels for 0%

profile of v1, /device:TPU:1, one launch (start us, length us, event | category | flops | bytes accessed | tf_op | source)
XLA Modules:
  0.0 444.4 jit_solution(15462017902587226464)
XLA Ops:
  1.5 14.5 %collective-permute-start = (f32[32,1,256]{2,0,1:T(8,128)S(1)}, f32[32,1,256]{2,0,1:T(8,128)S(1)}, u32[]{:S(2)}, u32[]{:S(2)}) collective-permute-start(f32[32,1,256]{2,0,1:T(8,128)S(1)} %get-tuple-element.30), channel_id=1, source_target_pairs={{16,0},{32,16},{48,32},{64,48},{80,64},{96,80},{112,96},{128,112},... | collective-permute-start | bytes 98312 | tf_op jit(solution)/shard_map/ppermute | solution.py:24
  16.0 1.9 collective-permute-start.2
  18.1 4.0 collective-permute-start.4
  22.1 1.9 collective-permute-start.1
  24.3 6.3 %collective-permute-done.1 = s32[1,256]{1,0:T(1,128)S(1)} collective-permute-done((s32[1,256]{1,0:T(1,128)S(1)}, s32[1,256]{1,0:T(1,128)S(1)}, u32[]{:S(2)}, u32[]{:S(2)}) %collective-permute-start.1) | collective-permute-done | bytes 1056 | tf_op jit(solution)/shard_map/ppermute | solution.py:13
  31.3 2.8 collective-permute-start.5
  34.6 1.9 collective-permute-start.3
  37.8 2.1 collective-permute-done.3
  41.3 2.0 fusion.44
  43.2 4.2 collective-permute-start.6
  47.4 1.9 collective-permute-start.7
  50.0 6.0 %collective-permute-done.7 = f32[32,1,256]{2,0,1:T(8,128)S(1)} collective-permute-done((f32[32,1,256]{2,0,1:T(8,128)S(1)}, f32[32,1,256]{2,0,1:T(8,128)S(1)}, u32[]{:S(2)}, u32[]{:S(2)}) %collective-permute-start.7) | collective-permute-done | bytes 32800 | tf_op jit(solution)/shard_map/ppermute | solution.py:23
  58.7 2.6 collective-permute-start.9
  62.7 10.5 %collective-permute-start.8 = (f32[32,34,1]{1,0,2:T(8,128)S(1)}, f32[32,34,1]{1,0,2:T(8,128)}, u32[]{:S(2)}, u32[]{:S(2)}) collective-permute-start(f32[32,34,1]{1,0,2:T(8,128)S(1)} %copy.129), channel_id=1, source_target_pairs={{1,0},{2,1},{3,2},{4,3},{5,4},{6,5},{7,6},{8,7},{9,8},{10,9},{11,1... | collective-permute-start | bytes 13064 | tf_op jit(solution)/shard_map/ppermute | solution.py:24
  73.2 3.1 broadcast_multiply_fusion.1
  77.6 2.1 copy.92
  79.7 2.9 broadcast_multiply_fusion
  82.6 1.9 collective-permute-start.10
  84.6 3.4 collective-permute-start.11
  87.9 5.2 %collective-permute-done.11 = f32[32,1,256]{2,0,1:T(8,128)S(1)} collective-permute-done((f32[32,1,256]{2,0,1:T(8,128)S(1)}, f32[32,1,256]{2,0,1:T(8,128)S(1)}, u32[]{:S(2)}, u32[]{:S(2)}) %collective-permute-start.11) | collective-permute-done | bytes 32800 | tf_op jit(solution)/shard_map/ppermute | solution.py:23
  93.9 2.0 collective-permute-start.13
  96.3 10.8 %collective-permute-start.12 = (f32[32,34,1]{1,0,2:T(8,128)S(1)}, f32[32,34,1]{1,0,2:T(8,128)S(1)}, u32[]{:S(2)}, u32[]{:S(2)}) collective-permute-start(f32[32,34,1]{1,0,2:T(8,128)S(1)} %copy.131), channel_id=1, source_target_pairs={{1,0},{2,1},{3,2},{4,3},{5,4},{6,5},{7,6},{8,7},{9,8},{10,9},{11,1... | collective-permute-start | bytes 13064 | tf_op jit(solution)/shard_map/ppermute | solution.py:24
  109.9 6.0 %fusion.32 = f32[32,32,256]{2,0,1:T(8,128)S(1)} fusion(f32[32,34,1]{2,0,1:T(8,128)} %copy.100, f32[32,1,256]{2,0,1:T(8,128)S(1)} %collective-permute-done.10, f32[32,32,256]{2,0,1:T(8,128)} %copy-done.1, f32[32,1,256]{2,0,1:T(8,128)S(1)} %collective-permute-done.11, f32[32,34,1]{2,0,1:T(8,128)} %copy.98, f32[32,32,256]{2,0,1:T(8,128)} %get-tuple-element.8, ...), kind=kLoop, calls=%fused_computation.59 | loop fusion | flops 9175040 | bytes 4539392 | tf_op jit(solution)/shard_map/sub | solution.py:91
  115.9 1.9 collective-permute-start.14
  117.8 3.4 collective-permute-start.15
  121.2 5.2 %collective-permute-done.15 = f32[32,1,256]{2,0,1:T(8,128)S(1)} collective-permute-done((f32[32,1,256]{2,0,1:T(8,128)S(1)}, f32[32,1,256]{2,0,1:T(8,128)S(1)}, u32[]{:S(2)}, u32[]{:S(2)}) %collective-permute-start.15) | collective-permute-done | bytes 32800 | tf_op jit(solution)/shard_map/ppermute | solution.py:23
  131.6 2.0 copy.133
  133.6 11.0 %collective-permute-start.16 = (f32[32,34,1]{1,0,2:T(8,128)}, f32[32,34,1]{1,0,2:T(8,128)}, u32[]{:S(2)}, u32[]{:S(2)}) collective-permute-start(f32[32,34,1]{1,0,2:T(8,128)} %copy.133), channel_id=1, source_target_pairs={{1,0},{2,1},{3,2},{4,3},{5,4},{6,5},{7,6},{8,7},{9,8},{10,9},{11,1... | collective-permute-start | bytes 13064 | tf_op jit(solution)/shard_map/ppermute | solution.py:24
  144.6 2.1 fusion.4
  146.8 2.1 copy.106
  148.8 2.1 copy.104
  150.9 2.4 fusion.24
  153.3 1.9 collective-permute-start.18
  155.3 3.4 collective-permute-start.19
  158.7 2.2 fusion.3
  160.9 3.0 collective-permute-done.19
  169.0 2.0 copy.135
  171.0 10.8 %collective-permute-start.20 = (f32[32,34,1]{1,0,2:T(8,128)}, f32[32,34,1]{1,0,2:T(8,128)}, u32[]{:S(2)}, u32[]{:S(2)}) collective-permute-start(f32[32,34,1]{1,0,2:T(8,128)} %copy.135), channel_id=1, source_target_pairs={{1,0},{2,1},{3,2},{4,3},{5,4},{6,5},{7,6},{8,7},{9,8},{10,9},{11,1... | collective-permute-start | bytes 13064 | tf_op jit(solution)/shard_map/ppermute | solution.py:24
  181.9 2.1 fusion.2
  184.0 2.1 copy.112
  186.1 2.1 copy.110
  188.1 1.9 fusion.16
  190.1 1.9 collective-permute-start.23
  192.0 7.5 %collective-permute-start.22 = (f32[32,1,256]{2,0,1:T(8,128)S(1)}, f32[32,1,256]{2,0,1:T(8,128)S(1)}, u32[]{:S(2)}, u32[]{:S(2)}) collective-permute-start(f32[32,1,256]{2,0,1:T(8,128)S(1)} %get-tuple-element.19), channel_id=1, source_target_pairs={{16,0},{32,16},{48,32},{64,48},{80,64},{96,80},{112,96},{128,112},... | collective-permute-start | bytes 98312 | tf_op jit(solution)/shard_map/ppermute | solution.py:24
  199.5 2.1 fusion.1
  201.7 2.2 fusion
  203.8 125.3 %psum.14 = f32[5,64,32]{2,1,0:T(8,128)S(1)} all-reduce(f32[5,64,32]{2,1,0:T(8,128)S(1)} %fusion), channel_id=1, replica_groups=mesh['sx'=32,'sy'=16] {'sx'}, use_global_device_ids=true, to_apply=%region_0.1 | all-reduce | flops 10240 | bytes 81920 | tf_op jit(solution)/shard_map/psum | solution.py:95
  329.1 114.4 %psum.15 = f32[5,64,32]{2,1,0:T(8,128)S(1)} all-reduce(f32[5,64,32]{2,1,0:T(8,128)S(1)} %psum.14), channel_id=1, replica_groups=mesh['sx'=32,'sy'=16] {'sy'}, use_global_device_ids=true, to_apply=%region_1.2 | all-reduce | flops 10240 | bytes 81920 | tf_op jit(solution)/shard_map/psum | solution.py:95
  (116 shorter events, 26.9 us)
Async XLA Ops:
  0.0 144.6 %copy-start = (bf16[64,32,256]{2,1,0:T(8,128)(2,1)S(1)}, bf16[64,32,256]{2,1,0:T(8,128)(2,1)}, u32[]{:S(2)}) copy-start(bf16[64,32,256]{2,1,0:T(8,128)(2,1)} %param.7) | copy-start | bytes 3145732
  0.0 17.9 %copy-start.5 = (s32[2,32,256]{2,1,0:T(8,128)S(1)}, s32[2,32,256]{2,1,0:T(8,128)}, u32[]{:S(2)}) copy-start(s32[2,32,256]{2,1,0:T(8,128)} %param.10) | copy-start | bytes 196612
  1.5 29.1 %collective-permute-start = (f32[32,1,256]{2,0,1:T(8,128)S(1)}, f32[32,1,256]{2,0,1:T(8,128)S(1)}, u32[]{:S(2)}, u32[]{:S(2)}) collective-permute-start(f32[32,1,256]{2,0,1:T(8,128)S(1)} %get-tuple-element.30), channel_id=1, source_target_pairs={{16,0},{32,16},{48,32},{64,48},{80,64},{96,80},{112,96},{128,112},... | collective-permute-start | bytes 98312 | tf_op jit(solution)/shard_map/ppermute | solution.py:24
  16.0 14.6 %collective-permute-start.2 = (f32[32,1,256]{2,0,1:T(8,128)S(1)}, f32[32,1,256]{2,0,1:T(8,128)S(1)}, u32[]{:S(2)}, u32[]{:S(2)}) collective-permute-start(f32[32,1,256]{2,0,1:T(8,128)S(1)} %get-tuple-element.29), channel_id=1, source_target_pairs={{0,16},{16,32},{32,48},{48,64},{64,80},{80,96},{96,112},{112,128},... | collective-permute-start | bytes 98312 | tf_op jit(solution)/shard_map/ppermute | solution.py:23
  18.1 6.0 %collective-permute-start.4 = (s32[32,1]{0,1:T(1,128)S(1)}, s32[32,1]{0,1:T(1,128)S(1)}, u32[]{:S(2)}, u32[]{:S(2)}) collective-permute-start(s32[32,1]{0,1:T(1,128)S(1)} %bitcast.60), channel_id=1, source_target_pairs={{0,1},{1,2},{2,3},{3,4},{4,5},{5,6},{6,7},{7,8},{8,9},{9,10},{10,1... | collective-permute-start | bytes 392 | tf_op jit(solution)/shard_map/ppermute | solution.py:13
  22.1 8.5 %collective-permute-start.1 = (s32[1,256]{1,0:T(1,128)S(1)}, s32[1,256]{1,0:T(1,128)S(1)}, u32[]{:S(2)}, u32[]{:S(2)}) collective-permute-start(s32[1,256]{1,0:T(1,128)S(1)} %slice_bitcast_fusion.1), channel_id=1, source_target_pairs={{0,16},{16,32},{32,48},{48,64},{64,80},{80,96},{96,112},{112,128},... | collective-permute-start | bytes 3080 | tf_op jit(solution)/shard_map/ppermute | solution.py:13
  31.3 5.1 %collective-permute-start.5 = (f32[32,34,1]{1,0,2:T(8,128)S(1)}, f32[32,34,1]{1,0,2:T(8,128)S(1)}, u32[]{:S(2)}, u32[]{:S(2)}) collective-permute-start(f32[32,34,1]{1,0,2:T(8,128)S(1)} %copy.128), channel_id=1, source_target_pairs={{0,1},{1,2},{2,3},{3,4},{4,5},{5,6},{6,7},{7,8},{8,9},{9,10},{10,1... | collective-permute-start | bytes 13064 | tf_op jit(solution)/shard_map/ppermute | solution.py:23
  34.6 5.3 %collective-permute-start.3 = (f32[32,34,1]{1,0,2:T(8,128)S(1)}, f32[32,34,1]{1,0,2:T(8,128)S(1)}, u32[]{:S(2)}, u32[]{:S(2)}) collective-permute-start(f32[32,34,1]{1,0,2:T(8,128)S(1)} %copy.127), channel_id=1, source_target_pairs={{1,0},{2,1},{3,2},{4,3},{5,4},{6,5},{7,6},{8,7},{9,8},{10,9},{11,1... | collective-permute-start | bytes 13064 | tf_op jit(solution)/shard_map/ppermute | solution.py:24
  41.3 8.1 %copy-start.24 = (f32[4]{0:T(128)S(1)}, f32[4]{0:T(128)}, u32[]{:S(2)}) copy-start(f32[4]{0:T(128)} %param.9) | copy-start | bytes 52
  43.2 36.5 %copy-start.3 = (f32[32,32,256]{2,0,1:T(8,128)}, f32[32,32,256]{2,0,1:T(8,128)S(1)}, u32[]{:S(2)}) copy-start(f32[32,32,256]{2,0,1:T(8,128)S(1)} %fusion.44) | copy-start | bytes 3145732
  43.2 6.7 %collective-permute-start.6 = (f32[32,1,256]{2,0,1:T(8,128)S(1)}, f32[32,1,256]{2,0,1:T(8,128)S(1)}, u32[]{:S(2)}, u32[]{:S(2)}) collective-permute-start(f32[32,1,256]{2,0,1:T(8,128)S(1)} %get-tuple-element.28), channel_id=1, source_target_pairs={{16,0},{32,16},{48,32},{64,48},{80,64},{96,80},{112,96},{128,112},... | collective-permute-start | bytes 98312 | tf_op jit(solution)/shard_map/ppermute | solution.py:24
  47.4 8.6 %collective-permute-start.7 = (f32[32,1,256]{2,0,1:T(8,128)S(1)}, f32[32,1,256]{2,0,1:T(8,128)S(1)}, u32[]{:S(2)}, u32[]{:S(2)}) collective-permute-start(f32[32,1,256]{2,0,1:T(8,128)S(1)} %get-tuple-element.27), channel_id=1, source_target_pairs={{0,16},{16,32},{32,48},{48,64},{64,80},{80,96},{96,112},{112,128},... | collective-permute-start | bytes 98312 | tf_op jit(solution)/shard_map/ppermute | solution.py:23
  50.0 29.7 %copy-start.6 = (f32[32,1,256]{2,0,1:T(8,128)}, f32[32,1,256]{2,0,1:T(8,128)S(1)}, u32[]{:S(2)}) copy-start(f32[32,1,256]{2,0,1:T(8,128)S(1)} %collective-permute-done.6) | copy-start | bytes 98308
  56.0 23.7 %copy-start.8 = (f32[32,1,256]{2,0,1:T(8,128)}, f32[32,1,256]{2,0,1:T(8,128)S(1)}, u32[]{:S(2)}) copy-start(f32[32,1,256]{2,0,1:T(8,128)S(1)} %collective-permute-done.7) | copy-start | bytes 98308
  57.3 15.9 %copy-start.23 = (s32[32,256]{1,0:T(8,128)S(1)}, s32[32,256]{1,0:T(8,128)}, u32[]{:S(2)}) copy-start(s32[32,256]{1,0:T(8,128)} %param.8) | copy-start | bytes 98308
  58.7 17.6 %collective-permute-start.9 = (f32[32,34,1]{1,0,2:T(8,128)S(1)}, f32[32,34,1]{1,0,2:T(8,128)S(1)}, u32[]{:S(2)}, u32[]{:S(2)}) collective-permute-start(f32[32,34,1]{1,0,2:T(8,128)S(1)} %copy.130), channel_id=1, source_target_pairs={{0,1},{1,2},{2,3},{3,4},{4,5},{5,6},{6,7},{7,8},{8,9},{9,10},{10,1... | collective-permute-start | bytes 13064 | tf_op jit(solution)/shard_map/ppermute | solution.py:23
  62.7 14.9 %collective-permute-start.8 = (f32[32,34,1]{1,0,2:T(8,128)S(1)}, f32[32,34,1]{1,0,2:T(8,128)}, u32[]{:S(2)}, u32[]{:S(2)}) collective-permute-start(f32[32,34,1]{1,0,2:T(8,128)S(1)} %copy.129), channel_id=1, source_target_pairs={{1,0},{2,1},{3,2},{4,3},{5,4},{6,5},{7,6},{8,7},{9,8},{10,9},{11,1... | collective-permute-start | bytes 13064 | tf_op jit(solution)/shard_map/ppermute | solution.py:24
  82.6 10.6 %copy-start.1 = (f32[32,32,256]{2,0,1:T(8,128)}, f32[32,32,256]{2,0,1:T(8,128)S(1)}, u32[]{:S(2)}) copy-start(f32[32,32,256]{2,0,1:T(8,128)S(1)} %get-tuple-element.7) | copy-start | bytes 3145732
  82.6 5.3 %collective-permute-start.10 = (f32[32,1,256]{2,0,1:T(8,128)S(1)}, f32[32,1,256]{2,0,1:T(8,128)S(1)}, u32[]{:S(2)}, u32[]{:S(2)}) collective-permute-start(f32[32,1,256]{2,0,1:T(8,128)S(1)} %get-tuple-element.26), channel_id=1, source_target_pairs={{16,0},{32,16},{48,32},{64,48},{80,64},{96,80},{112,96},{128,112},... | collective-permute-start | bytes 98312 | tf_op jit(solution)/shard_map/ppermute | solution.py:24
  84.6 8.6 %collective-permute-start.11 = (f32[32,1,256]{2,0,1:T(8,128)S(1)}, f32[32,1,256]{2,0,1:T(8,128)S(1)}, u32[]{:S(2)}, u32[]{:S(2)}) collective-permute-start(f32[32,1,256]{2,0,1:T(8,128)S(1)} %get-tuple-element.25), channel_id=1, source_target_pairs={{0,16},{16,32},{32,48},{48,64},{64,80},{80,96},{96,112},{112,128},... | collective-permute-start | bytes 98312 | tf_op jit(solution)/shard_map/ppermute | solution.py:23
  87.9 21.9 %copy-start.10 = (f32[32,1,256]{2,0,1:T(8,128)}, f32[32,1,256]{2,0,1:T(8,128)S(1)}, u32[]{:S(2)}) copy-start(f32[32,1,256]{2,0,1:T(8,128)S(1)} %collective-permute-done.10) | copy-start | bytes 98308
  93.1 16.8 %copy-start.12 = (f32[32,1,256]{2,0,1:T(8,128)}, f32[32,1,256]{2,0,1:T(8,128)S(1)}, u32[]{:S(2)}) copy-start(f32[32,1,256]{2,0,1:T(8,128)S(1)} %collective-permute-done.11) | copy-start | bytes 98308
  93.9 16.0 %copy-start.22 = (f32[32,256]{1,0:T(8,128)S(1)}, f32[32,256]{1,0:T(8,128)}, u32[]{:S(2)}) copy-start(f32[32,256]{1,0:T(8,128)} %get-tuple-element.5) | copy-start | bytes 98308
  93.9 13.3 %collective-permute-start.13 = (f32[32,34,1]{1,0,2:T(8,128)S(1)}, f32[32,34,1]{1,0,2:T(8,128)S(1)}, u32[]{:S(2)}, u32[]{:S(2)}) collective-permute-start(f32[32,34,1]{1,0,2:T(8,128)S(1)} %copy.132), channel_id=1, source_target_pairs={{0,1},{1,2},{2,3},{3,4},{4,5},{5,6},{6,7},{7,8},{8,9},{9,10},{10,1... | collective-permute-start | bytes 13064 | tf_op jit(solution)/shard_map/ppermute | solution.py:23
  96.3 12.2 %collective-permute-start.12 = (f32[32,34,1]{1,0,2:T(8,128)S(1)}, f32[32,34,1]{1,0,2:T(8,128)S(1)}, u32[]{:S(2)}, u32[]{:S(2)}) collective-permute-start(f32[32,34,1]{1,0,2:T(8,128)S(1)} %copy.131), channel_id=1, source_target_pairs={{1,0},{2,1},{3,2},{4,3},{5,4},{6,5},{7,6},{8,7},{9,8},{10,9},{11,1... | collective-permute-start | bytes 13064 | tf_op jit(solution)/shard_map/ppermute | solution.py:24
  115.9 5.3 %collective-permute-start.14 = (f32[32,1,256]{2,0,1:T(8,128)S(1)}, f32[32,1,256]{2,0,1:T(8,128)S(1)}, u32[]{:S(2)}, u32[]{:S(2)}) collective-permute-start(f32[32,1,256]{2,0,1:T(8,128)S(1)} %get-tuple-element.24), channel_id=1, source_target_pairs={{16,0},{32,16},{48,32},{64,48},{80,64},{96,80},{112,96},{128,112},... | collective-permute-start | bytes 98312 | tf_op jit(solution)/shard_map/ppermute | solution.py:24
  117.8 8.6 %collective-permute-start.15 = (f32[32,1,256]{2,0,1:T(8,128)S(1)}, f32[32,1,256]{2,0,1:T(8,128)S(1)}, u32[]{:S(2)}, u32[]{:S(2)}) collective-permute-start(f32[32,1,256]{2,0,1:T(8,128)S(1)} %get-tuple-element.23), channel_id=1, source_target_pairs={{0,16},{16,32},{32,48},{48,64},{64,80},{80,96},{96,112},{112,128},... | collective-permute-start | bytes 98312 | tf_op jit(solution)/shard_map/ppermute | solution.py:23
  121.2 5.3 %copy-start.14 = (f32[32,1,256]{2,0,1:T(8,128)}, f32[32,1,256]{2,0,1:T(8,128)S(1)}, u32[]{:S(2)}) copy-start(f32[32,1,256]{2,0,1:T(8,128)S(1)} %collective-permute-done.14) | copy-start | bytes 98308
  128.1 16.5 %copy-start.4 = (f32[32,32,256]{2,0,1:T(8,128)S(1)}, f32[32,32,256]{2,0,1:T(8,128)}, u32[]{:S(2)}) copy-start(f32[32,32,256]{2,0,1:T(8,128)} %copy-done.3) | copy-start | bytes 3145732
  128.1 16.5 %copy-start.7 = (f32[32,1,256]{2,0,1:T(8,128)S(1)}, f32[32,1,256]{2,0,1:T(8,128)}, u32[]{:S(2)}) copy-start(f32[32,1,256]{2,0,1:T(8,128)} %copy-done.6) | copy-start | bytes 98308
  128.1 16.5 %copy-start.9 = (f32[32,1,256]{2,0,1:T(8,128)S(1)}, f32[32,1,256]{2,0,1:T(8,128)}, u32[]{:S(2)}) copy-start(f32[32,1,256]{2,0,1:T(8,128)} %copy-done.8) | copy-start | bytes 98308
  129.6 17.1 %collective-permute-start.17 = (f32[32,34,1]{1,0,2:T(8,128)S(1)}, f32[32,34,1]{1,0,2:T(8,128)}, u32[]{:S(2)}, u32[]{:S(2)}) collective-permute-start(f32[32,34,1]{1,0,2:T(8,128)S(1)} %copy.134), channel_id=1, source_target_pairs={{0,1},{1,2},{2,3},{3,4},{4,5},{5,6},{6,7},{7,8},{8,9},{9,10},{10,1... | collective-permute-start | bytes 13064 | tf_op jit(solution)/shard_map/ppermute | solution.py:23
  133.6 15.3 %collective-permute-start.16 = (f32[32,34,1]{1,0,2:T(8,128)}, f32[32,34,1]{1,0,2:T(8,128)}, u32[]{:S(2)}, u32[]{:S(2)}) collective-permute-start(f32[32,34,1]{1,0,2:T(8,128)} %copy.133), channel_id=1, source_target_pairs={{1,0},{2,1},{3,2},{4,3},{5,4},{6,5},{7,6},{8,7},{9,8},{10,9},{11,1... | collective-permute-start | bytes 13064 | tf_op jit(solution)/shard_map/ppermute | solution.py:24
  150.9 7.7 %copy-start.2 = (f32[32,32,256]{2,0,1:T(8,128)S(1)}, f32[32,32,256]{2,0,1:T(8,128)}, u32[]{:S(2)}) copy-start(f32[32,32,256]{2,0,1:T(8,128)} %copy-done.1) | copy-start | bytes 3145732
  150.9 7.8 %copy-start.11 = (f32[32,1,256]{2,0,1:T(8,128)S(1)}, f32[32,1,256]{2,0,1:T(8,128)}, u32[]{:S(2)}) copy-start(f32[32,1,256]{2,0,1:T(8,128)} %copy-done.10) | copy-start | bytes 98308
  150.9 7.8 %copy-start.13 = (f32[32,1,256]{2,0,1:T(8,128)S(1)}, f32[32,1,256]{2,0,1:T(8,128)}, u32[]{:S(2)}) copy-start(f32[32,1,256]{2,0,1:T(8,128)} %copy-done.12) | copy-start | bytes 98308
  153.3 7.5 %collective-permute-start.18 = (f32[32,1,256]{2,0,1:T(8,128)S(1)}, f32[32,1,256]{2,0,1:T(8,128)S(1)}, u32[]{:S(2)}, u32[]{:S(2)}) collective-permute-start(f32[32,1,256]{2,0,1:T(8,128)S(1)} %get-tuple-element.22), channel_id=1, source_target_pairs={{16,0},{32,16},{48,32},{64,48},{80,64},{96,80},{112,96},{128,112},... | collective-permute-start | bytes 98312 | tf_op jit(solution)/shard_map/ppermute | solution.py:24
  155.3 8.6 %collective-permute-start.19 = (f32[32,1,256]{2,0,1:T(8,128)S(1)}, f32[32,1,256]{2,0,1:T(8,128)S(1)}, u32[]{:S(2)}, u32[]{:S(2)}) collective-permute-start(f32[32,1,256]{2,0,1:T(8,128)S(1)} %get-tuple-element.21), channel_id=1, source_target_pairs={{0,16},{16,32},{32,48},{48,64},{64,80},{80,96},{96,112},{112,128},... | collective-permute-start | bytes 98312 | tf_op jit(solution)/shard_map/ppermute | solution.py:23
  160.8 3.1 copy-start.18
  165.7 16.2 %copy-start.15 = (f32[32,1,256]{2,0,1:T(8,128)S(1)}, f32[32,1,256]{2,0,1:T(8,128)}, u32[]{:S(2)}) copy-start(f32[32,1,256]{2,0,1:T(8,128)} %copy-done.14) | copy-start | bytes 98308
  165.7 16.2 %copy-start.17 = (f32[32,1,256]{2,0,1:T(8,128)S(1)}, f32[32,1,256]{2,0,1:T(8,128)}, u32[]{:S(2)}) copy-start(f32[32,1,256]{2,0,1:T(8,128)} %copy-done.16) | copy-start | bytes 98308
  167.1 16.9 %collective-permute-start.21 = (f32[32,34,1]{1,0,2:T(8,128)S(1)}, f32[32,34,1]{1,0,2:T(8,128)}, u32[]{:S(2)}, u32[]{:S(2)}) collective-permute-start(f32[32,34,1]{1,0,2:T(8,128)S(1)} %copy.136), channel_id=1, source_target_pairs={{0,1},{1,2},{2,3},{3,4},{4,5},{5,6},{6,7},{7,8},{8,9},{9,10},{10,1... | collective-permute-start | bytes 13064 | tf_op jit(solution)/shard_map/ppermute | solution.py:23
  171.0 15.0 %collective-permute-start.20 = (f32[32,34,1]{1,0,2:T(8,128)}, f32[32,34,1]{1,0,2:T(8,128)}, u32[]{:S(2)}, u32[]{:S(2)}) collective-permute-start(f32[32,34,1]{1,0,2:T(8,128)} %copy.135), channel_id=1, source_target_pairs={{1,0},{2,1},{3,2},{4,3},{5,4},{6,5},{7,6},{8,7},{9,8},{10,9},{11,1... | collective-permute-start | bytes 13064 | tf_op jit(solution)/shard_map/ppermute | solution.py:24
  183.9 4.2 copy-start.19
  184.0 4.2 copy-start.21
  190.1 11.5 %collective-permute-start.23 = (f32[32,1,256]{2,0,1:T(8,128)S(1)}, f32[32,1,256]{2,0,1:T(8,128)S(1)}, u32[]{:S(2)}, u32[]{:S(2)}) collective-permute-start(f32[32,1,256]{2,0,1:T(8,128)S(1)} %get-tuple-element.20), channel_id=1, source_target_pairs={{0,16},{16,32},{32,48},{48,64},{64,80},{80,96},{96,112},{112,128},... | collective-permute-start | bytes 98312 | tf_op jit(solution)/shard_map/ppermute | solution.py:23
  192.0 9.6 %collective-permute-start.22 = (f32[32,1,256]{2,0,1:T(8,128)S(1)}, f32[32,1,256]{2,0,1:T(8,128)S(1)}, u32[]{:S(2)}, u32[]{:S(2)}) collective-permute-start(f32[32,1,256]{2,0,1:T(8,128)S(1)} %get-tuple-element.19), channel_id=1, source_target_pairs={{16,0},{32,16},{48,32},{64,48},{80,64},{96,80},{112,96},{128,112},... | collective-permute-start | bytes 98312 | tf_op jit(solution)/shard_map/ppermute | solution.py:24
  201.6 241.9 %copy-start.25 = (s32[5]{0:T(128)S(1)}, s32[5]{0:T(128)}, u32[]{:S(2)}) copy-start(s32[5]{0:T(128)} %param.11) | copy-start | bytes 64
  (2 other events, 1.2 us)
